TPU v7x, 32 devices: a whole 2x2x4 slice. The times are simulated.
32 devices in a mesh: gx: 8 (over z, y), gy: 4 (over x, core).
Axes of the slice: x: 2, y: 2, z: 4, core: 2. Of those that a mesh axis runs over, the one named last changes fastest.
Arguments:
- tokens: bfloat16 [48, 24, 8, 384], P('gx', 'gy'), may hold values from -6 to 6
- upstream: bfloat16 [48, 24, 8, 384], P('gx', 'gy'), may hold values from -41 to 41
- window_labels: int32 [48, 24, 8], P('gx', 'gy'), may hold values from 0 to 2
- ln1_gain: float32 [384], replicated, may hold values from 0.5 to 1.5
- w_qkv: bfloat16 [384, 1152], replicated, as said below
- w_proj: bfloat16 [384, 384], replicated, may hold values from -0.3125 to 0.3125
- ln2_gain: float32 [384], replicated, may hold values from 0.5 to 1.5
- w_fc1: bfloat16 [384, 1536], replicated, may hold values from -0.3125 to 0.3125
- b_fc1: float32 [1536], replicated, may hold values from -3 to 3
- w_fc2: bfloat16 [1536, 384], replicated, may hold values from -0.15625 to 0.15625
Outputs:
- d_tokens: bfloat16 [48, 24, 8, 384], P('gx', 'gy')
- g_ln1: float32 [384], replicated
- g_qkv: bfloat16 [384, 1152], replicated
- g_proj: bfloat16 [384, 384], replicated
- g_ln2: float32 [384], replicated
- g_fc1: bfloat16 [384, 1536], replicated
- g_bfc1: float32 [1536], replicated
- g_fc2: bfloat16 [1536, 384], replicated
Inputs may be any that keep to these rules, and one draw needn't show every extreme that they name: `w_qkv`: entries at most 28 / sqrt(384) in magnitude.
All inputs are finite; a program needn't handle non-finite values.
Results may differ from a plain program's by a relative error of at most 0.019.
Values may be sent and summed in bfloat16 or wider, within the bound.
No kernel may reach another device: no remote copies, remote signals or barrier semaphores. Data moves between devices by JAX's collectives and lax.ppermute only.
A program may use at most 128 MiB of HBM per device.

v0:
```python
import math
import jax
import jax.numpy as jnp
from jax import lax
from jax.sharding import PartitionSpec as P

HD = 32
WZ = 8
EPS = 1e-05
CUBIC = 0.044715
ROOT_TWO_PI = math.sqrt(2.0 / math.pi)


def shifted(shard, axis, by):
    size = lax.axis_size(axis)
    return lax.ppermute(shard, axis, [(i, (i + by) % size) for i in range(size)])


def row_stats(values):
    row_mean = jnp.mean(values, axis=-1, keepdims=True)
    center = values - row_mean
    variance = jnp.mean(center * center, axis=-1, keepdims=True)
    inv_std = lax.rsqrt(variance + EPS)
    return (center * inv_std, inv_std)


def norm_back(incoming, normed, inv_std, gain_vec):
    scaled = incoming * gain_vec
    first_mean = jnp.mean(scaled, axis=-1, keepdims=True)
    second_mean = jnp.mean(scaled * normed, axis=-1, keepdims=True)
    flat_terms = (incoming * normed).reshape(-1, incoming.shape[-1])
    return (inv_std * (scaled - first_mean - normed * second_mean), jnp.sum(flat_terms, axis=0))


def gelu_pair(preact):
    cubic_arg = ROOT_TWO_PI * (preact + CUBIC * preact * preact * preact)
    tanh_value = jnp.tanh(cubic_arg)
    gelu_value = 0.5 * preact * (1.0 + tanh_value)
    gelu_slope = 0.5 * (1.0 + tanh_value) + 0.5 * preact * (
        1.0 - tanh_value * tanh_value
    ) * ROOT_TWO_PI * (1.0 + 3.0 * CUBIC * preact * preact)
    return (gelu_value, gelu_slope)


def to_windows(grid_tile, win_depth):
    tile_x, tile_y, tile_z = grid_tile.shape[:3]
    trailing = grid_tile.shape[3:]
    blocks = tile_z // win_depth
    shaped = grid_tile.reshape((tile_x, tile_y, blocks, win_depth) + trailing)
    axes_order = (2, 0, 1, 3) + tuple(range(4, 4 + len(trailing)))
    return shaped.transpose(axes_order).reshape((blocks, tile_x * tile_y * win_depth) + trailing)


def from_windows(win_rows, tile_x, tile_y, win_depth):
    blocks = win_rows.shape[0]
    trailing = win_rows.shape[2:]
    shaped = win_rows.reshape((blocks, tile_x, tile_y, win_depth) + trailing)
    axes_order = (1, 2, 0, 3) + tuple(range(4, 4 + len(trailing)))
    return shaped.transpose(axes_order).reshape((tile_x, tile_y, blocks * win_depth) + trailing)


def roll_ahead(grid_tile, dim_x):
    half_size = grid_tile.shape[dim_x] // 2
    arrived = shifted(lax.slice_in_dim(grid_tile, 0, half_size, axis=dim_x), "gx", -1)
    grid_tile = jnp.concatenate(
        (lax.slice_in_dim(grid_tile, half_size, grid_tile.shape[dim_x], axis=dim_x), arrived),
        axis=dim_x,
    )
    dim_y = dim_x + 1
    half_size = grid_tile.shape[dim_y] // 2
    arrived = shifted(lax.slice_in_dim(grid_tile, 0, half_size, axis=dim_y), "gy", -1)
    grid_tile = jnp.concatenate(
        (lax.slice_in_dim(grid_tile, half_size, grid_tile.shape[dim_y], axis=dim_y), arrived),
        axis=dim_y,
    )
    return jnp.roll(grid_tile, -(WZ // 2), axis=dim_x + 2)


def unroll_wide(grid_tile):
    grid_tile = jnp.roll(grid_tile, WZ // 2, axis=2)
    size_x = grid_tile.shape[0]
    keep_x = size_x - size_x // 2
    arrived = shifted(grid_tile[keep_x:].astype(jnp.bfloat16), "gx", 1).astype(jnp.float32)
    grid_tile = jnp.concatenate((arrived, grid_tile[:keep_x]), axis=0)
    size_y = grid_tile.shape[1]
    keep_y = size_y - size_y // 2
    arrived = shifted(grid_tile[:, keep_y:].astype(jnp.bfloat16), "gy", 1).astype(jnp.float32)
    return jnp.concatenate((arrived, grid_tile[:, :keep_y]), axis=1)


def attend_forward(h_rows, region_codes, w_qkv, w_proj):
    blocks, length, model_width = h_rows.shape
    head_count = model_width // HD
    score_scale = HD ** (-0.5)
    packed = jnp.dot(
        h_rows.reshape(-1, model_width), w_qkv, preferred_element_type=jnp.float32
    ).astype(jnp.bfloat16)
    packed = packed.reshape(blocks, length, 3, head_count, HD)
    queries = packed[:, :, 0]
    key_part = packed[:, :, 1]
    val_part = packed[:, :, 2]
    allowed = (region_codes[:, :, None] == region_codes[:, None, :])[:, None]
    scores = (
        jnp.einsum("bqhe,bkhe->bhqk", queries, key_part, preferred_element_type=jnp.float32)
        * score_scale
    )
    scores = jnp.where(allowed, scores, -1e30)
    highest = jnp.max(scores, axis=-1, keepdims=True)
    exp_scores = jnp.exp(scores - highest)
    probs = exp_scores / jnp.sum(exp_scores, axis=-1, keepdims=True)
    probs_low = probs.astype(jnp.bfloat16)
    head_mix = jnp.einsum(
        "bhqk,bkhe->bqhe", probs_low, val_part, preferred_element_type=jnp.float32
    ).astype(jnp.bfloat16)
    head_mix = head_mix.reshape(blocks * length, model_width)
    attn_out = jnp.dot(head_mix, w_proj, preferred_element_type=jnp.float32).reshape(
        blocks, length, model_width
    )
    return (attn_out, (queries, key_part, val_part, probs, probs_low, head_mix))


def attend_backward(grad_rows, saved, h_rows, w_qkv, w_proj):
    queries, key_part, val_part, probs, probs_low, head_mix = saved
    blocks, length, model_width = grad_rows.shape
    head_count = model_width // HD
    score_scale = HD ** (-0.5)
    flat_grad = grad_rows.reshape(-1, model_width)
    grad_proj = jnp.dot(head_mix.T, flat_grad, preferred_element_type=jnp.float32)
    grad_mix = jnp.dot(flat_grad, w_proj.T, preferred_element_type=jnp.float32).astype(jnp.bfloat16)
    grad_mix = grad_mix.reshape(blocks, length, head_count, HD)
    grad_probs = jnp.einsum(
        "bqhe,bkhe->bhqk", grad_mix, val_part, preferred_element_type=jnp.float32
    )
    grad_val = jnp.einsum(
        "bhqk,bqhe->bkhe", probs_low, grad_mix, preferred_element_type=jnp.float32
    )
    grad_scores = probs * (grad_probs - jnp.sum(probs * grad_probs, axis=-1, keepdims=True))
    grad_low = (grad_scores * score_scale).astype(jnp.bfloat16)
    grad_query = jnp.einsum(
        "bhqk,bkhe->bqhe", grad_low, key_part, preferred_element_type=jnp.float32
    )
    grad_key = jnp.einsum("bhqk,bqhe->bkhe", grad_low, queries, preferred_element_type=jnp.float32)
    grad_packed = (
        jnp.stack((grad_query, grad_key, grad_val), axis=2)
        .astype(jnp.bfloat16)
        .reshape(-1, 3 * model_width)
    )
    grad_qkv = jnp.dot(
        h_rows.reshape(-1, model_width).T, grad_packed, preferred_element_type=jnp.float32
    )
    grad_input = jnp.dot(grad_packed, w_qkv.T, preferred_element_type=jnp.float32).reshape(
        blocks, length, model_width
    )
    return (grad_input, grad_qkv, grad_proj)


def mlp_backward(wide_tok, attn_out, up_tok, ln2_gain, w_fc1, b_fc1, w_fc2):
    model_width = wide_tok.shape[-1]
    lead_shape = wide_tok.shape[:-1]
    resid_mid = (wide_tok + attn_out).astype(jnp.bfloat16)
    normed, inv_std = row_stats(resid_mid.astype(jnp.float32))
    hidden_in = (normed * ln2_gain).astype(jnp.bfloat16).reshape(-1, model_width)
    preact = jnp.dot(hidden_in, w_fc1, preferred_element_type=jnp.float32) + b_fc1
    gelu_value, gelu_slope = gelu_pair(preact)
    hidden = gelu_value.astype(jnp.bfloat16)
    flat_up = up_tok.reshape(-1, model_width)
    grad_fc2 = jnp.dot(hidden.T, flat_up, preferred_element_type=jnp.float32)
    grad_pre = (jnp.dot(flat_up, w_fc2.T, preferred_element_type=jnp.float32) * gelu_slope).astype(
        jnp.bfloat16
    )
    grad_bias = jnp.sum(grad_pre.astype(jnp.float32), axis=0)
    grad_fc1 = jnp.dot(hidden_in.T, grad_pre, preferred_element_type=jnp.float32)
    grad_norm = jnp.dot(grad_pre, w_fc1.T, preferred_element_type=jnp.float32).reshape(
        lead_shape + (model_width,)
    )
    grad_mid, grad_gain2 = norm_back(grad_norm, normed, inv_std, ln2_gain)
    grad_res = up_tok.astype(jnp.float32) + grad_mid
    return (grad_res, (grad_gain2, grad_fc1, grad_bias, grad_fc2))


def body(tokens, upstream, window_labels, ln1_gain, w_qkv, w_proj, ln2_gain, w_fc1, b_fc1, w_fc2):
    tile_x, tile_y, tile_z, model_width = tokens.shape
    last_x = lax.axis_index("gx") == lax.axis_size("gx") - 1
    last_y = lax.axis_index("gy") == lax.axis_size("gy") - 1
    wrap_x = (last_x & (jnp.arange(tile_x) >= tile_x - tile_x // 2)).astype(jnp.int32)
    wrap_y = (last_y & (jnp.arange(tile_y) >= tile_y - tile_y // 2)).astype(jnp.int32)
    wrap_z = (jnp.arange(tile_z) >= tile_z - WZ // 2).astype(jnp.int32)
    code_tile = (
        window_labels * 8
        + wrap_x[:, None, None] * 4
        + wrap_y[None, :, None] * 2
        + wrap_z[None, None, :]
    )
    region_codes = to_windows(code_tile, WZ)
    wide_tok = tokens.astype(jnp.float32)
    normed_first, inv_first = row_stats(wide_tok)
    h_first = (normed_first * ln1_gain).astype(jnp.bfloat16)
    h_rows = to_windows(roll_ahead(h_first, 0), WZ)
    attn_rows, saved = attend_forward(h_rows, region_codes, w_qkv, w_proj)
    attn_tile = unroll_wide(from_windows(attn_rows, tile_x, tile_y, WZ))
    grad_res, mlp_grads = mlp_backward(wide_tok, attn_tile, upstream, ln2_gain, w_fc1, b_fc1, w_fc2)
    grad_attn = grad_res.astype(jnp.bfloat16)
    grad_rows = to_windows(roll_ahead(grad_attn, 0), WZ)
    input_rows, grad_qkv, grad_proj = attend_backward(grad_rows, saved, h_rows, w_qkv, w_proj)
    grad_first = unroll_wide(from_windows(input_rows, tile_x, tile_y, WZ))
    grad_tok, grad_gain1 = norm_back(grad_first, normed_first, inv_first, ln1_gain)
    result = (grad_res + grad_tok).astype(jnp.bfloat16)
    grad_gain2, grad_fc1, grad_bias, grad_fc2 = mlp_grads
    local_grads = (grad_gain1, grad_qkv, grad_proj, grad_gain2, grad_fc1, grad_bias, grad_fc2)
    param_total = 0
    for grad_term in local_grads:
        param_total = param_total + math.prod(grad_term.shape)
    summed = lax.psum(
        (
            local_grads[0],
            local_grads[1],
            local_grads[2],
            local_grads[3],
            local_grads[4],
            local_grads[5],
            local_grads[6],
        ),
        ("gx", "gy"),
    )
    square_sum = jnp.zeros((), jnp.float32)
    for grad_term in summed:
        square_sum = square_sum + jnp.sum(grad_term * grad_term)
    factor = math.sqrt(param_total) * lax.rsqrt(square_sum)
    scaled = tuple((grad_term * factor for grad_term in summed))
    return (
        result,
        scaled[0],
        scaled[1].astype(jnp.bfloat16),
        scaled[2].astype(jnp.bfloat16),
        scaled[3],
        scaled[4].astype(jnp.bfloat16),
        scaled[5],
        scaled[6].astype(jnp.bfloat16),
    )


def solution(mesh):
    return jax.shard_map(
        body,
        mesh=mesh,
        in_specs=(
            P("gx", "gy", None, None),
            P("gx", "gy", None, None),
            P("gx", "gy", None),
            P(),
            P(),
            P(),
            P(),
            P(),
            P(),
            P(),
        ),
        out_specs=(P("gx", "gy", None, None), P(), P(), P(), P(), P(), P(), P()),
        check_vma=False,
    )
```

profile of v0, /device:TPU:0, one launch (start us, length us, event | category | flops | bytes accessed | tf_op | source)
XLA Modules:
  0.0 288.3 jit_solution(15074106265206905131)
XLA Ops:
  10.7 6.1 %collective-permute-start = (bf16[3,6,8,384]{3,2,1,0:T(8,128)(2,1)S(1)}, bf16[3,6,8,384]{3,2,1,0:T(8,128)(2,1)S(1)}, u32[]{:S(2)}, u32[]{:S(2)}) collective-permute-start(bf16[3,6,8,384]{3,2,1,0:T(8,128)(2,1)S(1)} %get-tuple-element.33), channel_id=1, source_target_pairs={{0,28},{4,0},{8,4},{12,8},{16,12},{20,16},{24,20},{28,24},{1,29},{... | collective-permute-start | bytes 331784 | tf_op jit(solution)/shard_map/ppermute | solution.py:16
  19.4 2.2 collective-permute-done.1
  22.8 4.2 %fusion.108 = (f32[12,288]{1,0:T(8,128)S(1)}, f32[12,288,288]{1,2,0:T(8,128)}) fusion(pred[288,288]{0,1:T(8,128)(4,1)S(1)} %broadcast_compare_fusion, bf16[1,288,3,12,32]{1,4,3,2,0:T(8,128)(2,1)S(1)} %bitcast.100), kind=kOutput, calls=%fused_computation.164 | convolution fusion | flops 67682592 | bytes 4695552 | tf_op jit(solution)/shard_map/sub | solution.py:109
  27.0 3.1 %fusion.36 = bf16[12,32,288]{2,1,0:T(8,128)(2,1)S(1)} fusion(bf16[1,288,3,12,32]{1,4,3,2,0:T(8,128)(2,1)S(1)} %bitcast.101, f32[12,288,288]{1,2,0:T(8,128)} %get-tuple-element.35, f32[12,288]{1,0:T(8,128)S(1)} %get-tuple-element.34), kind=kOutput, calls=%fused_computation.43 | convolution fusion | flops 65802240 | bytes 4521984 | tf_op jit(solution)/shard_map/bhqk,bkhe->bqhe/dot_general | solution.py:112
  32.9 7.8 %collective-permute-done.2 = bf16[3,6,8,384]{3,2,1,0:T(8,128)(2,1)S(1)} collective-permute-done((bf16[3,6,8,384]{3,2,1,0:T(8,128)(2,1)S(1)}, bf16[3,6,8,384]{3,2,1,0:T(8,128)(2,1)S(1)}, u32[]{:S(2)}, u32[]{:S(2)}) %collective-permute-start.2) | collective-permute-done | bytes 110624 | tf_op jit(solution)/shard_map/ppermute | solution.py:16
  41.6 3.6 %collective-permute-done.3 = bf16[6,3,8,384]{3,2,1,0:T(8,128)(2,1)S(1)} collective-permute-done((bf16[6,3,8,384]{3,2,1,0:T(8,128)(2,1)S(1)}, bf16[6,3,8,384]{3,2,1,0:T(8,128)(2,1)S(1)}, u32[]{:S(2)}, u32[]{:S(2)}) %collective-permute-start.3) | collective-permute-done | bytes 110624 | tf_op jit(solution)/shard_map/ppermute | solution.py:16
  46.7 2.0 convert_reduce_fusion
  51.6 2.1 collective-permute-start.4
  53.8 4.1 %fusion.39 = f32[1536,384]{1,0:T(8,128)} fusion(bf16[288,384]{1,0:T(8,128)(2,1)S(1)} %bitcast.110, f32[288,1536]{1,0:T(8,128)} %copy-done.7), kind=kOutput, calls=%fused_computation.45 | convolution fusion | flops 343719936 | bytes 4349952 | tf_op jit(solution)/shard_map/dot_general | solution.py:167
  58.1 2.2 fusion.111
  61.8 4.2 %fusion.33 = bf16[1,288,1,12,32]{1,4,3,2,0:T(8,128)(2,1)} fusion(bf16[288,12,32]{0,2,1:T(8,128)(2,1)} %bitcast.105, f32[12,288,288]{1,2,0:T(8,128)} %get-tuple-element.35, f32[12,288]{1,0:T(8,128)} %copy-done.27), kind=kOutput, calls=%fused_computation.42 | convolution fusion | flops 65691648 | bytes 4437504 | tf_op jit(solution)/shard_map/bhqk,bqhe->bkhe/dot_general | solution.py:134
  66.0 3.2 %fusion.80 = f32[12,288,288]{1,2,0:T(8,128)} fusion(bf16[288,12,32]{0,2,1:T(8,128)(2,1)S(1)} %bitcast.106, bf16[1,288,3,12,32]{1,4,3,2,0:T(8,128)(2,1)S(1)} %bitcast.102), kind=kOutput, calls=%fused_computation.104 | convolution fusion | flops 63700992 | bytes 4571136 | tf_op jit(solution)/shard_map/bqhe,bkhe->bhqk/dot_general | solution.py:131
  69.3 9.4 %fusion.30 = bf16[1,288,1,12,32]{1,4,3,2,0:T(8,128)(2,1)} fusion(f32[12,288,288]{1,2,0:T(8,128)} %fusion.80, bf16[1,288,3,12,32]{1,4,3,2,0:T(8,128)(2,1)S(1)} %bitcast.103, f32[12,288,288]{1,2,0:T(8,128)} %get-tuple-element.35, f32[12,288]{1,0:T(8,128)} %copy-done.27), kind=kOutput, calls=%fused_computation.41 | convolution fusion | flops 70672032 | bytes 21798912 | tf_op jit(solution)/shard_map/bhqk,bqhe->bkhe/dot_general | solution.py:142
  78.7 9.4 %fusion.27 = bf16[1,288,1,12,32]{1,4,3,2,0:T(8,128)(2,1)} fusion(f32[12,288,288]{1,2,0:T(8,128)} %fusion.80, bf16[1,288,3,12,32]{1,4,3,2,0:T(8,128)(2,1)S(1)} %bitcast.104, f32[12,288,288]{1,2,0:T(8,128)} %get-tuple-element.35, f32[12,288]{1,0:T(8,128)} %copy-done.27), kind=kOutput, calls=%fused_computation.40 | convolution fusion | flops 70672032 | bytes 21798912 | tf_op jit(solution)/shard_map/bhqk,bkhe->bqhe/dot_general | solution.py:139
  89.4 1.9 fusion.109
  92.5 4.4 %copy.36 = bf16[1,288,3,12,32]{4,3,2,1,0:T(8,128)(2,1)} copy(bf16[1,288,3,12,32]{1,4,3,2,0:T(8,128)(2,1)S(1)} %maximum_convert_fusion) | data formatting | bytes 1327104 | tf_op jit(solution)/shard_map/convert_element_type | solution.py:145
  96.9 5.2 %convert_element_type.139 = bf16[6,6,8,1152]{3,2,1,0:T(8,128)(2,1)} reshape(bf16[1,288,3,12,32]{4,3,2,1,0:T(8,128)(2,1)} %copy.36) | data formatting | bytes 1327104 | tf_op jit(solution)/shard_map/convert_element_type | solution.py:145
  104.0 10.6 %collective-permute-done.6 = bf16[3,6,8,384]{3,2,1,0:T(8,128)(2,1)S(1)} collective-permute-done((bf16[3,6,8,384]{3,2,1,0:T(8,128)(2,1)S(1)}, bf16[3,6,8,384]{3,2,1,0:T(8,128)(2,1)S(1)}, u32[]{:S(2)}, u32[]{:S(2)}) %collective-permute-start.6) | collective-permute-done | bytes 110624 | tf_op jit(solution)/shard_map/ppermute | solution.py:16
  115.8 4.9 %collective-permute-done.7 = bf16[6,3,8,384]{3,2,1,0:T(8,128)(2,1)S(1)} collective-permute-done((bf16[6,3,8,384]{3,2,1,0:T(8,128)(2,1)S(1)}, bf16[6,3,8,384]{3,2,1,0:T(8,128)(2,1)S(1)}, u32[]{:S(2)}, u32[]{:S(2)}) %collective-permute-start.7) | collective-permute-done | bytes 110624 | tf_op jit(solution)/shard_map/ppermute | solution.py:16
  121.0 38.2 %all-reduce = (f32[384]{0:T(512)S(1)}, f32[384]{0:T(512)S(1)}, f32[1536]{0:T(1024)S(1)}) all-reduce(f32[384]{0:T(512)S(1)} %get-tuple-element.10, f32[384]{0:T(512)} %get-tuple-element.8, f32[1536]{0:T(1024)} %get-tuple-element.38), channel_id=1, replica_groups=mesh['gx'=8,'gy'=4] {'gx','gy'}, use_global_device_ids=true, to_apply=%region_12.13 | all-reduce | flops 2304 | bytes 18432 | tf_op jit(solution)/shard_map/psum | solution.py:213
  162.2 98.9 %all-reduce.4.cloned.1.call-done = (f32[384,1152]{1,0:T(8,128)}, f32[384,384]{1,0:T(8,128)}, f32[384,1536]{1,0:T(8,128)}, f32[1536,384]{1,0:T(8,128)}) async-done(((f32[384,1152]{1,0:T(8,128)}, f32[384,384]{1,0:T(8,128)}, f32[384,1536]{1,0:T(8,128)}, f32[1536,384]{1,0:T(8,128)}), (f32[384,1152]{1,0:T(8,128)}, f32[384,384]{1,0:T(8,128)}, f32[384,1536]{1,0:T(8,128)}, ...) | async-done | bytes 7077904 | tf_op jit(solution)/shard_map/psum | solution.py:213
  261.1 2.7 multiply_reduce_fusion.3
  263.8 1.8 multiply_reduce_fusion.4
  273.4 2.6 multiply_convert_fusion.3
  (136 shorter events, 34.3 us)
Async XLA Ops:
  7.2 38.7 %copy-start = (bf16[384,1536]{1,0:T(8,128)(2,1)S(1)}, bf16[384,1536]{1,0:T(8,128)(2,1)}, u32[]{:S(2)}) copy-start(bf16[384,1536]{1,0:T(8,128)(2,1)} %param.17) | copy-start | bytes 3538948
  7.2 14.6 %copy-start.5 = (bf16[384,1152]{1,0:T(8,128)(2,1)S(1)}, bf16[384,1152]{1,0:T(8,128)(2,1)}, u32[]{:S(2)}) copy-start(bf16[384,1152]{1,0:T(8,128)(2,1)} %param.14) | copy-start | bytes 2654212
  7.2 253.9 %all-reduce.4.cloned.1.call-start = ((), (), s32[]{:S(2)}) async-start(), calls=%async_computation | async-start | bytes 14155776 | tf_op jit(solution)/shard_map/psum | solution.py:213
  10.7 8.4 %collective-permute-start = (bf16[3,6,8,384]{3,2,1,0:T(8,128)(2,1)S(1)}, bf16[3,6,8,384]{3,2,1,0:T(8,128)(2,1)S(1)}, u32[]{:S(2)}, u32[]{:S(2)}) collective-permute-start(bf16[3,6,8,384]{3,2,1,0:T(8,128)(2,1)S(1)} %get-tuple-element.33), channel_id=1, source_target_pairs={{0,28},{4,0},{8,4},{12,8},{16,12},{20,16},{24,20},{28,24},{1,29},{... | collective-permute-start | bytes 331784 | tf_op jit(solution)/shard_map/ppermute | solution.py:16
  19.2 2.5 collective-permute-start.1
  22.8 4.2 %copy-start.8 = (bf16[288,1152]{0,1:T(8,128)(2,1)}, bf16[288,1152]{0,1:T(8,128)(2,1)S(1)}, u32[]{:S(2)}) copy-start(bf16[288,1152]{0,1:T(8,128)(2,1)S(1)} %copy.29) | copy-start | bytes 1990660
  32.0 13.3 %copy-start.4 = (bf16[6,6,8,384]{3,2,1,0:T(8,128)(2,1)S(1)}, bf16[6,6,8,384]{3,2,1,0:T(8,128)(2,1)}, u32[]{:S(2)}) copy-start(bf16[6,6,8,384]{3,2,1,0:T(8,128)(2,1)} %param.10) | copy-start | bytes 663556
  32.4 13.4 %copy-start.19 = (f32[384]{0:T(512)S(1)}, f32[384]{0:T(512)}, u32[]{:S(2)}) copy-start(f32[384]{0:T(512)} %param.16) | copy-start | bytes 4612
  32.5 13.5 %copy-start.21 = (f32[1536]{0:T(1024)S(1)}, f32[1536]{0:T(1024)}, u32[]{:S(2)}) copy-start(f32[1536]{0:T(1024)} %param.18) | copy-start | bytes 18436
  32.5 8.2 %collective-permute-start.2 = (bf16[3,6,8,384]{3,2,1,0:T(8,128)(2,1)S(1)}, bf16[3,6,8,384]{3,2,1,0:T(8,128)(2,1)S(1)}, u32[]{:S(2)}, u32[]{:S(2)}) collective-permute-start(bf16[3,6,8,384]{3,2,1,0:T(8,128)(2,1)S(1)} %fusion.85), channel_id=1, source_target_pairs={{0,4},{4,8},{8,12},{12,16},{16,20},{20,24},{24,28},{28,0},{1,5},{5... | collective-permute-start | bytes 331784 | tf_op jit(solution)/shard_map/ppermute | solution.py:16
  40.8 4.5 %collective-permute-start.3 = (bf16[6,3,8,384]{3,2,1,0:T(8,128)(2,1)S(1)}, bf16[6,3,8,384]{3,2,1,0:T(8,128)(2,1)S(1)}, u32[]{:S(2)}, u32[]{:S(2)}) collective-permute-start(bf16[6,3,8,384]{3,2,1,0:T(8,128)(2,1)S(1)} %slice.203), channel_id=1, source_target_pairs={{0,1},{1,2},{2,3},{3,0},{4,5},{5,6},{6,7},{7,4},{8,9},{9,10},{10,1... | collective-permute-start | bytes 331784 | tf_op jit(solution)/shard_map/ppermute | solution.py:16
  51.6 6.5 %copy-start.16 = (bf16[288,1536]{1,0:T(8,128)(2,1)S(1)}, bf16[288,1536]{1,0:T(8,128)(2,1)}, u32[]{:S(2)}) copy-start(bf16[288,1536]{1,0:T(8,128)(2,1)} %copy-done.15) | copy-start | bytes 2654212
  51.6 6.2 %collective-permute-start.4 = (bf16[3,6,8,384]{3,2,1,0:T(8,128)(2,1)S(1)}, bf16[3,6,8,384]{3,2,1,0:T(8,128)(2,1)S(1)}, u32[]{:S(2)}, u32[]{:S(2)}) collective-permute-start(bf16[3,6,8,384]{3,2,1,0:T(8,128)(2,1)S(1)} %get-tuple-element.29), channel_id=1, source_target_pairs={{0,28},{4,0},{8,4},{12,8},{16,12},{20,16},{24,20},{28,24},{1,29},{... | collective-permute-start | bytes 331784 | tf_op jit(solution)/shard_map/ppermute | solution.py:16
  57.8 2.6 collective-permute-start.5
  96.9 5.2 %copy-start.6 = (bf16[384,1152]{1,0:T(8,128)(2,1)S(1)}, bf16[384,1152]{1,0:T(8,128)(2,1)}, u32[]{:S(2)}) copy-start(bf16[384,1152]{1,0:T(8,128)(2,1)} %param.14) | copy-start | bytes 2654212
  103.7 16.9 %copy-start.20 = (f32[384]{0:T(512)S(1)}, f32[384]{0:T(512)}, u32[]{:S(2)}) copy-start(f32[384]{0:T(512)} %param.13) | copy-start | bytes 4612
  103.7 57.4 %copy-start.18 = (bf16[6,6,8,384]{3,2,1,0:T(8,128)(2,1)S(1)}, bf16[6,6,8,384]{3,2,1,0:T(8,128)(2,1)}, u32[]{:S(2)}) copy-start(bf16[6,6,8,384]{3,2,1,0:T(8,128)(2,1)} %param.11) | copy-start | bytes 663556
  103.9 10.6 %collective-permute-start.6 = (bf16[3,6,8,384]{3,2,1,0:T(8,128)(2,1)S(1)}, bf16[3,6,8,384]{3,2,1,0:T(8,128)(2,1)S(1)}, u32[]{:S(2)}, u32[]{:S(2)}) collective-permute-start(bf16[3,6,8,384]{3,2,1,0:T(8,128)(2,1)S(1)} %fusion.83), channel_id=1, source_target_pairs={{0,4},{4,8},{8,12},{12,16},{16,20},{20,24},{24,28},{28,0},{1,5},{5... | collective-permute-start | bytes 331784 | tf_op jit(solution)/shard_map/ppermute | solution.py:16
  114.6 6.0 %collective-permute-start.7 = (bf16[6,3,8,384]{3,2,1,0:T(8,128)(2,1)S(1)}, bf16[6,3,8,384]{3,2,1,0:T(8,128)(2,1)S(1)}, u32[]{:S(2)}, u32[]{:S(2)}) collective-permute-start(bf16[6,3,8,384]{3,2,1,0:T(8,128)(2,1)S(1)} %slice.202), channel_id=1, source_target_pairs={{0,1},{1,2},{2,3},{3,0},{4,5},{5,6},{6,7},{7,4},{8,9},{9,10},{10,1... | collective-permute-start | bytes 331784 | tf_op jit(solution)/shard_map/ppermute | solution.py:16
  261.1 4.5 %copy-start.2 = (f32[384,1536]{1,0:T(8,128)S(1)}, f32[384,1536]{1,0:T(8,128)}, u32[]{:S(2)}) copy-start(f32[384,1536]{1,0:T(8,128)} %get-tuple-element.18) | copy-start | bytes 7077892
  261.1 5.7 %copy-start.1 = (f32[1536,384]{1,0:T(8,128)S(1)}, f32[1536,384]{1,0:T(8,128)}, u32[]{:S(2)}) copy-start(f32[1536,384]{1,0:T(8,128)} %get-tuple-element.19) | copy-start | bytes 7077892
  265.6 7.2 %copy-start.25 = (f32[384]{0:T(512)S(1)}, f32[384]{0:T(512)}, u32[]{:S(2)}) copy-start(f32[384]{0:T(512)} %copy-done.24) | copy-start | bytes 4612
  268.1 9.7 %copy-start.23 = (f32[384]{0:T(512)S(1)}, f32[384]{0:T(512)}, u32[]{:S(2)}) copy-start(f32[384]{0:T(512)} %copy-done.22) | copy-start | bytes 4612
  272.8 5.6 %copy-start.3 = (f32[384,1536]{1,0:T(8,128)S(1)}, f32[384,1536]{1,0:T(8,128)}, u32[]{:S(2)}) copy-start(f32[384,1536]{1,0:T(8,128)} %get-tuple-element.18) | copy-start | bytes 7077892
  (13 other events, 31.3 us)
Sparse Core Ops, SparseCore 0:
  92.6 168.4 all-reduce.3
where the time goes:
time: 289 us; the launch traced here: 288 us
  waiting for transfers between devices  130 us (45%)
  matrix products  49 us (17%)
  blocking collectives  38.2 us (13%)
  other arithmetic  27 us (9%)
  between operations  19.3 us (7%)
  local copies, waits for them, and re-layouts  14.4 us (5%)
  starting transfers between devices  11 us (4%)
    psum x1, waiting for transfers between devices, body(): lax.psum((local_grads[0], local_grads[1], local_grads[2], local_grads[3],...  98.9 us
    psum x1, blocking collectives, body(): lax.psum((local_grads[0], local_grads[1], local_grads[2], local_grads[3],...  38.2 us
    ppermute x8, waiting for transfers between devices, shifted(): lax.ppermute(shard, axis, [(i, (i + by) % size) for i in range(size)])  30.6 us
    ppermute x8, starting transfers between devices, shifted(): lax.ppermute(shard, axis, [(i, (i + by) % size) for i in range(size)])  10.9 us
    convert_element_type x2, local copies, waits for them, and re-layouts, attend_backward(): grad_packed = jnp.stack((grad_query, grad_key, grad_val), axis=2).astype(...  9.59 us
    dot_general x1, matrix products, attend_backward(): jnp.einsum('bhqk,bqhe->bkhe', grad_low, queries, preferred_element_type=j...  9.44 us
    dot_general x1, matrix products, attend_backward(): jnp.einsum('bhqk,bkhe->bqhe', grad_low, key_part, preferred_element_type=...  9.35 us
    reduce_sum x7, other arithmetic, body(): square_sum = square_sum + jnp.sum(grad_term * grad_term)  8.87 us
  transfers between devices with their start and end apart: 9, of which 8 were waited for; matrix products, arithmetic and copies ran while one was open for 8% of the time, Pallas kernels for 0%

commit v1 on v0

--- a/solution.py
+++ b/solution.py
@@ -211,16 +211,19 @@
     for grad_term in local_grads:
         param_total = param_total + math.prod(grad_term.shape)
     summed = lax.psum(
-        (
-            local_grads[0],
-            local_grads[1],
-            local_grads[2],
-            local_grads[3],
-            local_grads[4],
-            local_grads[5],
-            local_grads[6],
+        lax.psum(
+            (
+                local_grads[0],
+                local_grads[1],
+                local_grads[2],
+                local_grads[3],
+                local_grads[4],
+                local_grads[5],
+                local_grads[6],
+            ),
+            "gy",
         ),
-        ("gx", "gy"),
+        "gx",
     )
     square_sum = jnp.zeros((), jnp.float32)
     for grad_term in summed:

time: 289 us -> 497 us (1.72)
  waiting for transfers between devices: 130 us -> 329 us
  blocking collectives: 38.2 us -> 47.3 us
    psum x0 -> x1, waiting for transfers between devices: none -> 167 us  [body(): lax.psum(lax.psum((local_grads[0], local_grads[1], local_grads[2], local_...]
    psum x0 -> x1, blocking collectives: none -> 36.4 us  [body(): lax.psum(lax.psum((local_grads[0], local_grads[1], local_grads[2], local_...]
    psum x1, waiting for transfers between devices: 98.9 us -> 134 us  [body(): lax.psum((local_grads[0], local_grads[1], local_grads[2], local_grads[3],...]
    psum x1, blocking collectives: 38.2 us -> 10.9 us  [body(): lax.psum((local_grads[0], local_grads[1], local_grads[2], local_grads[3],...]
  transfers between devices with their start and end apart: 9 -> 10, of which waited for: 8 -> 9; matrix products, arithmetic and copies ran while one was open for 8% -> 4% of each run, Pallas kernels for 0% -> 0%
where the time goes in v1:
time: 497 us; the launch traced here: 496 us
  waiting for transfers between devices  329 us (66%)
  matrix products  49.2 us (10%)
  blocking collectives  47.3 us (10%)
  other arithmetic  26.4 us (5%)
  between operations  19.2 us (4%)
  local copies, waits for them, and re-layouts  14.2 us (3%)
  starting transfers between devices  11.3 us (2%)
    psum x1, waiting for transfers between devices, body(): lax.psum(lax.psum((local_grads[0], local_grads[1], local_grads[2], local_...  167 us
    psum x1, waiting for transfers between devices, body(): lax.psum((local_grads[0], local_grads[1], local_grads[2], local_grads[3],...  134 us
    psum x1, blocking collectives, body(): lax.psum(lax.psum((local_grads[0], local_grads[1], local_grads[2], local_...  36.4 us
    ppermute x8, waiting for transfers between devices, shifted(): lax.ppermute(shard, axis, [(i, (i + by) % size) for i in range(size)])  28.3 us
    ppermute x8, starting transfers between devices, shifted(): lax.ppermute(shard, axis, [(i, (i + by) % size) for i in range(size)])  11.2 us
    psum x1, blocking collectives, body(): lax.psum((local_grads[0], local_grads[1], local_grads[2], local_grads[3],...  10.9 us
  transfers between devices with their start and end apart: 10, of which 9 were waited for; matrix products, arithmetic and copies ran while one was open for 4% of the time, Pallas kernels for 0%

profile of v1, /device:TPU:0, one launch (start us, length us, event | category | flops | bytes accessed | tf_op | source)
XLA Modules:
  0.0 496.4 jit_solution(4262973085192381928)
XLA Ops:
  10.7 6.1 %collective-permute-start = (bf16[3,6,8,384]{3,2,1,0:T(8,128)(2,1)S(1)}, bf16[3,6,8,384]{3,2,1,0:T(8,128)(2,1)S(1)}, u32[]{:S(2)}, u32[]{:S(2)}) collective-permute-start(bf16[3,6,8,384]{3,2,1,0:T(8,128)(2,1)S(1)} %get-tuple-element.40), channel_id=1, source_target_pairs={{0,28},{4,0},{8,4},{12,8},{16,12},{20,16},{24,20},{28,24},{1,29},{... | collective-permute-start | bytes 331784 | tf_op jit(solution)/shard_map/ppermute | solution.py:16
  19.4 2.2 collective-permute-done.1
  22.8 4.2 fusion.108
  27.0 3.1 fusion.36
  32.9 7.8 %collective-permute-done.2 = bf16[3,6,8,384]{3,2,1,0:T(8,128)(2,1)S(1)} collective-permute-done((bf16[3,6,8,384]{3,2,1,0:T(8,128)(2,1)S(1)}, bf16[3,6,8,384]{3,2,1,0:T(8,128)(2,1)S(1)}, u32[]{:S(2)}, u32[]{:S(2)}) %collective-permute-start.2) | collective-permute-done | bytes 110624 | tf_op jit(solution)/shard_map/ppermute | solution.py:16
  41.6 3.6 collective-permute-done.3
  46.7 2.0 convert_reduce_fusion
  51.2 2.1 collective-permute-start.4
  53.3 4.1 fusion.39
  57.6 2.2 fusion.111
  61.4 4.2 fusion.33
  65.6 3.2 fusion.80
  68.8 9.4 %fusion.30 = bf16[1,288,1,12,32]{1,4,3,2,0:T(8,128)(2,1)} fusion(f32[12,288,288]{1,2,0:T(8,128)} %fusion.80, bf16[1,288,3,12,32]{1,4,3,2,0:T(8,128)(2,1)S(1)} %bitcast.103, f32[12,288,288]{1,2,0:T(8,128)} %get-tuple-element.42, f32[12,288]{1,0:T(8,128)} %copy-done.27), kind=kOutput, calls=%fused_computation.41 | convolution fusion | flops 70672032 | bytes 21798912 | tf_op jit(solution)/shard_map/bhqk,bqhe->bkhe/dot_general | solution.py:142
  78.2 9.4 %fusion.27 = bf16[1,288,1,12,32]{1,4,3,2,0:T(8,128)(2,1)} fusion(f32[12,288,288]{1,2,0:T(8,128)} %fusion.80, bf16[1,288,3,12,32]{1,4,3,2,0:T(8,128)(2,1)S(1)} %bitcast.104, f32[12,288,288]{1,2,0:T(8,128)} %get-tuple-element.42, f32[12,288]{1,0:T(8,128)} %copy-done.27), kind=kOutput, calls=%fused_computation.40 | convolution fusion | flops 70672032 | bytes 21798912 | tf_op jit(solution)/shard_map/bhqk,bkhe->bqhe/dot_general | solution.py:139
  92.1 133.9 %all-reduce.9.cloned.1.call-done = (f32[384,1152]{1,0:T(8,128)}, f32[384,384]{1,0:T(8,128)}, f32[384,1536]{1,0:T(8,128)}, f32[1536,384]{1,0:T(8,128)}) async-done(((f32[384,1152]{1,0:T(8,128)}, f32[384,384]{1,0:T(8,128)}, f32[384,1536]{1,0:T(8,128)}, f32[1536,384]{1,0:T(8,128)}), (f32[384,1152]{1,0:T(8,128)}, f32[384,384]{1,0:T(8,128)}, f32[384,1536]{1,0:T(8,128)}, ...) | async-done | bytes 7077904 | tf_op jit(solution)/shard_map/psum | solution.py:214
  226.1 4.4 copy.36
  230.5 5.0 %convert_element_type.139 = bf16[6,6,8,1152]{3,2,1,0:T(8,128)(2,1)} reshape(bf16[1,288,3,12,32]{4,3,2,1,0:T(8,128)(2,1)} %copy.36) | data formatting | bytes 1327104 | tf_op jit(solution)/shard_map/convert_element_type | solution.py:145
  238.9 9.0 %collective-permute-done.6 = bf16[3,6,8,384]{3,2,1,0:T(8,128)(2,1)S(1)} collective-permute-done((bf16[3,6,8,384]{3,2,1,0:T(8,128)(2,1)S(1)}, bf16[3,6,8,384]{3,2,1,0:T(8,128)(2,1)S(1)}, u32[]{:S(2)}, u32[]{:S(2)}) %collective-permute-start.6) | collective-permute-done | bytes 110624 | tf_op jit(solution)/shard_map/ppermute | solution.py:16
  248.1 4.1 collective-permute-done.7
  252.6 10.9 %all-reduce.2 = (f32[384]{0:T(512)S(1)}, f32[384]{0:T(512)S(1)}, f32[1536]{0:T(1024)S(1)}) all-reduce(f32[384]{0:T(512)S(1)} %get-tuple-element.10, f32[384]{0:T(512)S(1)} %get-tuple-element.8, f32[1536]{0:T(1024)} %get-tuple-element.45), channel_id=1, replica_groups=mesh['gx'=8,'gy'=4] {'gy'}, use_global_device_ids=true, to_apply=%region_12.13 | all-reduce | flops 2304 | bytes 18432 | tf_op jit(solution)/shard_map/psum | solution.py:214
  263.5 36.4 %all-reduce = (f32[384]{0:T(512)S(1)}, f32[384]{0:T(512)S(1)}, f32[1536]{0:T(1024)S(1)}) all-reduce(f32[384]{0:T(512)S(1)} %get-tuple-element.20, f32[384]{0:T(512)S(1)} %get-tuple-element.21, f32[1536]{0:T(1024)S(1)} %get-tuple-element.22), channel_id=1, replica_groups=mesh['gx'=8,'gy'=4] {'gx'}, use_global_device_ids=true, to_apply=%region_13.14 | all-reduce | flops 2304 | bytes 18432 | tf_op jit(solution)/shard_map/psum | solution.py:213
  303.0 166.6 %all-reduce.7.cloned.1.call-done = (f32[384,1152]{1,0:T(8,128)}, f32[384,384]{1,0:T(8,128)}, f32[384,1536]{1,0:T(8,128)}, f32[1536,384]{1,0:T(8,128)}) async-done(((f32[384,1152]{1,0:T(8,128)}, f32[384,384]{1,0:T(8,128)}, f32[384,1536]{1,0:T(8,128)}, f32[1536,384]{1,0:T(8,128)}), (f32[384,1152]{1,0:T(8,128)}, f32[384,384]{1,0:T(8,128)}, f32[384,1536]{1,0:T(8,128)}, ...) | async-done | bytes 7077904 | tf_op jit(solution)/shard_map/psum | solution.py:213
  469.5 2.7 multiply_reduce_fusion.3
  481.6 2.6 multiply_convert_fusion.3
  (140 shorter events, 38.0 us)
Async XLA Ops:
  7.2 38.7 %copy-start = (bf16[384,1536]{1,0:T(8,128)(2,1)S(1)}, bf16[384,1536]{1,0:T(8,128)(2,1)}, u32[]{:S(2)}) copy-start(bf16[384,1536]{1,0:T(8,128)(2,1)} %param.17) | copy-start | bytes 3538948
  7.2 14.6 %copy-start.5 = (bf16[384,1152]{1,0:T(8,128)(2,1)S(1)}, bf16[384,1152]{1,0:T(8,128)(2,1)}, u32[]{:S(2)}) copy-start(bf16[384,1152]{1,0:T(8,128)(2,1)} %param.14) | copy-start | bytes 2654212
  7.2 218.8 %all-reduce.9.cloned.1.call-start = ((), (), s32[]{:S(2)}) async-start(), calls=%async_computation.1 | async-start | bytes 14155776 | tf_op jit(solution)/shard_map/psum | solution.py:214
  10.7 8.4 %collective-permute-start = (bf16[3,6,8,384]{3,2,1,0:T(8,128)(2,1)S(1)}, bf16[3,6,8,384]{3,2,1,0:T(8,128)(2,1)S(1)}, u32[]{:S(2)}, u32[]{:S(2)}) collective-permute-start(bf16[3,6,8,384]{3,2,1,0:T(8,128)(2,1)S(1)} %get-tuple-element.40), channel_id=1, source_target_pairs={{0,28},{4,0},{8,4},{12,8},{16,12},{20,16},{24,20},{28,24},{1,29},{... | collective-permute-start | bytes 331784 | tf_op jit(solution)/shard_map/ppermute | solution.py:16
  19.2 2.5 collective-permute-start.1
  32.0 13.3 %copy-start.4 = (bf16[6,6,8,384]{3,2,1,0:T(8,128)(2,1)S(1)}, bf16[6,6,8,384]{3,2,1,0:T(8,128)(2,1)}, u32[]{:S(2)}) copy-start(bf16[6,6,8,384]{3,2,1,0:T(8,128)(2,1)} %param.10) | copy-start | bytes 663556
  32.4 13.4 %copy-start.19 = (f32[384]{0:T(512)S(1)}, f32[384]{0:T(512)}, u32[]{:S(2)}) copy-start(f32[384]{0:T(512)} %param.16) | copy-start | bytes 4612
  32.5 13.5 %copy-start.21 = (f32[1536]{0:T(1024)S(1)}, f32[1536]{0:T(1024)}, u32[]{:S(2)}) copy-start(f32[1536]{0:T(1024)} %param.18) | copy-start | bytes 18436
  32.5 8.2 %collective-permute-start.2 = (bf16[3,6,8,384]{3,2,1,0:T(8,128)(2,1)S(1)}, bf16[3,6,8,384]{3,2,1,0:T(8,128)(2,1)S(1)}, u32[]{:S(2)}, u32[]{:S(2)}) collective-permute-start(bf16[3,6,8,384]{3,2,1,0:T(8,128)(2,1)S(1)} %fusion.85), channel_id=1, source_target_pairs={{0,4},{4,8},{8,12},{12,16},{16,20},{20,24},{24,28},{28,0},{1,5},{5... | collective-permute-start | bytes 331784 | tf_op jit(solution)/shard_map/ppermute | solution.py:16
  40.8 4.5 collective-permute-start.3
  51.1 6.5 %copy-start.16 = (bf16[288,1536]{1,0:T(8,128)(2,1)S(1)}, bf16[288,1536]{1,0:T(8,128)(2,1)}, u32[]{:S(2)}) copy-start(bf16[288,1536]{1,0:T(8,128)(2,1)} %copy-done.15) | copy-start | bytes 2654212
  51.2 6.2 %collective-permute-start.4 = (bf16[3,6,8,384]{3,2,1,0:T(8,128)(2,1)S(1)}, bf16[3,6,8,384]{3,2,1,0:T(8,128)(2,1)S(1)}, u32[]{:S(2)}, u32[]{:S(2)}) collective-permute-start(bf16[3,6,8,384]{3,2,1,0:T(8,128)(2,1)S(1)} %get-tuple-element.36), channel_id=1, source_target_pairs={{0,28},{4,0},{8,4},{12,8},{16,12},{20,16},{24,20},{28,24},{1,29},{... | collective-permute-start | bytes 331784 | tf_op jit(solution)/shard_map/ppermute | solution.py:16
  57.4 2.6 collective-permute-start.5
  92.1 377.4 %all-reduce.7.cloned.1.call-start = ((), (), s32[]{:S(2)}) async-start(), calls=%async_computation | async-start | bytes 14155776 | tf_op jit(solution)/shard_map/psum | solution.py:213
  230.5 5.0 %copy-start.6 = (bf16[384,1152]{1,0:T(8,128)(2,1)S(1)}, bf16[384,1152]{1,0:T(8,128)(2,1)}, u32[]{:S(2)}) copy-start(bf16[384,1152]{1,0:T(8,128)(2,1)} %param.14) | copy-start | bytes 2654212
  237.3 14.9 %copy-start.20 = (f32[384]{0:T(512)S(1)}, f32[384]{0:T(512)}, u32[]{:S(2)}) copy-start(f32[384]{0:T(512)} %param.13) | copy-start | bytes 4612
  237.3 64.5 %copy-start.18 = (bf16[6,6,8,384]{3,2,1,0:T(8,128)(2,1)S(1)}, bf16[6,6,8,384]{3,2,1,0:T(8,128)(2,1)}, u32[]{:S(2)}) copy-start(bf16[6,6,8,384]{3,2,1,0:T(8,128)(2,1)} %param.11) | copy-start | bytes 663556
  237.5 10.4 %collective-permute-start.6 = (bf16[3,6,8,384]{3,2,1,0:T(8,128)(2,1)S(1)}, bf16[3,6,8,384]{3,2,1,0:T(8,128)(2,1)S(1)}, u32[]{:S(2)}, u32[]{:S(2)}) collective-permute-start(bf16[3,6,8,384]{3,2,1,0:T(8,128)(2,1)S(1)} %fusion.83), channel_id=1, source_target_pairs={{0,4},{4,8},{8,12},{12,16},{16,20},{20,24},{24,28},{28,0},{1,5},{5... | collective-permute-start | bytes 331784 | tf_op jit(solution)/shard_map/ppermute | solution.py:16
  248.0 4.2 collective-permute-start.7
  469.5 4.5 copy-start.2
  469.5 5.7 %copy-start.1 = (f32[1536,384]{1,0:T(8,128)S(1)}, f32[1536,384]{1,0:T(8,128)}, u32[]{:S(2)}) copy-start(f32[1536,384]{1,0:T(8,128)} %get-tuple-element.19) | copy-start | bytes 7077892
  474.0 7.0 %copy-start.25 = (f32[384]{0:T(512)S(1)}, f32[384]{0:T(512)}, u32[]{:S(2)}) copy-start(f32[384]{0:T(512)} %copy-done.24) | copy-start | bytes 4612
  476.4 9.6 %copy-start.23 = (f32[384]{0:T(512)S(1)}, f32[384]{0:T(512)}, u32[]{:S(2)}) copy-start(f32[384]{0:T(512)} %copy-done.22) | copy-start | bytes 4612
  481.0 5.6 %copy-start.3 = (f32[384,1536]{1,0:T(8,128)S(1)}, f32[384,1536]{1,0:T(8,128)}, u32[]{:S(2)}) copy-start(f32[384,1536]{1,0:T(8,128)} %get-tuple-element.18) | copy-start | bytes 7077892
  (14 other events, 35.6 us)
Sparse Core Ops, SparseCore 0:
  92.2 133.8 all-reduce.8
  230.5 239.0 all-reduce.6
